TPU v7x, 128 devices: a whole 4x4x4 slice. The times are simulated.
128 devices in a mesh: dp: 8 (over z, x_hi), expert: 16 (over y, x_lo, core).
Axes of the slice: x: 4 (x_hi: 2, x_lo: 2; x = x_hi * 2 + x_lo), y: 4, z: 4, core: 2. Of those that a mesh axis runs over, the one named last changes fastest.
Arguments:
- activations: bfloat16 [16, 8192, 2048], P('expert', 'dp'), may hold values from -6 to 6
- grad_hidden: bfloat16 [16, 8192, 1536], P('expert', 'dp'), may hold values from -6 to 6
- counts: int32 [16, 8], P('expert', 'dp'), may hold values from 1 to 1024, as said below
- master: float32 [16, 2048, 1536], P('expert', 'dp'), may hold values from -0.125 to 0.125
- moment1: float32 [16, 2048, 1536], P('expert', 'dp'), may hold values from -3 to 3
- moment2: float32 [16, 2048, 1536], P('expert', 'dp'), may hold values from 0.01 to 1
- old_slot: int32 [16], replicated, may hold values from 0 to 15, each once
- new_slot: int32 [16], replicated, may hold values from 0 to 15, each once
Outputs:
- master_out: float32 [16, 2048, 1536], P('expert', 'dp')
- moment1_out: float32 [16, 2048, 1536], P('expert', 'dp')
- moment2_out: float32 [16, 2048, 1536], P('expert', 'dp')
- new_weight: bfloat16 [16, 2048, 1536], P('expert')
Inputs may be any that keep to these rules, and one draw needn't show every extreme that they name: `counts`: each entry is at most 1024, and some entry equals 1024.
All inputs are finite; a program needn't handle non-finite values.
Results may differ from a plain program's by a relative error of at most 0.0055.
Values may be sent and summed in bfloat16 or wider, within the bound.
A program may use at most 128 MiB of HBM per device.

v0:
```python
import math
import jax
import jax.numpy as jnp
from jax import lax
from jax.sharding import Mesh
from jax.sharding import PartitionSpec as P

EXPERT = ("expert_0", "expert_1", "expert_2")
beta_one = 0.9
beta_two = 0.95
learn_rate = 0.01
decay_rate = 0.1
adam_eps = 1e-08
step_number = 20


def in_blocks(value, dim, peers):
    dims = value.shape
    blocks = value.reshape(*dims[:dim], peers, dims[dim] // peers, *dims[dim + 1 :])
    return jnp.moveaxis(blocks, dim, 0)


def sent_and_summed(value, axis, dim):
    blocks = in_blocks(value, dim, lax.axis_size(axis))
    arrived = lax.all_to_all(blocks, axis, split_axis=0, concat_axis=0, tiled=True)
    return arrived.astype(jnp.float32).sum(axis=0)


def in_order(blocks, dim):
    blocks = jnp.moveaxis(blocks, 0, dim)
    dims = blocks.shape
    return blocks.reshape(*dims[:dim], dims[dim] * dims[dim + 1], *dims[dim + 2 :])


def exchange_in_order(blocks, axes, sequence):
    inside = blocks.shape[1:]
    whole = blocks.reshape(*(lax.axis_size(a) for a in axes), *inside)
    for k in sequence:
        whole = lax.all_to_all(whole, axes[k], k, k, tiled=True)
    return whole.reshape(-1, *inside)


def core_and_chips(value, groups, sequence, split_dim, concat_dim):
    peers = lax.axis_size(groups[0]) * lax.axis_size(groups[1])
    blocks = in_blocks(value, split_dim, peers)
    return in_order(exchange_in_order(blocks, groups, sequence), concat_dim)


def source_slots(old_slot, new_slot):
    slots = old_slot.shape[0]
    wanted = jnp.arange(slots, dtype=jnp.int32)
    picked = jnp.where(new_slot[None, :] == wanted[:, None], old_slot[None, :], 0)
    return jnp.sum(picked, axis=1)


def adamw(grads, master, moment1, moment2):
    first = beta_one * moment1 + (1.0 - beta_one) * grads
    second = beta_two * moment2 + (1.0 - beta_two) * grads * grads
    first_hat = first / (1.0 - beta_one**step_number)
    second_hat = second / (1.0 - beta_two**step_number)
    updated = master - learn_rate * (
        first_hat / (jnp.sqrt(second_hat) + adam_eps) + decay_rate * master
    )
    return (updated, first, second)


def on_device(activations, grad_hidden, counts, master, moment1, moment2, old_slot, new_slot):
    tokens_here = activations.shape[1]
    inputs = activations[0]
    row_index = jnp.arange(tokens_here, dtype=jnp.int32)
    cotangent = jnp.where(
        (row_index < counts[0, 0])[:, None], grad_hidden[0], jnp.zeros((), jnp.bfloat16)
    )
    grad_scale = 1.0 / math.sqrt(tokens_here * lax.axis_size("dp"))
    product = lax.dot_general(
        inputs, cotangent, (((0,), (0,)), ((), ())), preferred_element_type=jnp.float32
    )
    grads = sent_and_summed((product * grad_scale).astype(jnp.bfloat16), "dp", 0)
    updated, first, second = adamw(grads, master[0], moment1[0], moment2[0])
    weight_half = updated.astype(jnp.bfloat16)[None]
    source = source_slots(old_slot, new_slot)
    spread = core_and_chips(weight_half, (("expert_0", "expert_1"), "expert_2"), (1, 0), 1, 0)
    placed = lax.all_to_all(
        jnp.take(spread, source, axis=0), EXPERT, split_axis=0, concat_axis=1, tiled=True
    )
    moved = lax.all_gather(placed, "dp", axis=1, tiled=True)
    return (updated[None], first[None], second[None], moved)


def solution(mesh):
    finer = Mesh(
        mesh.devices.reshape(mesh.shape["dp"], 4, 2, 2), ("dp", "expert_0", "expert_1", "expert_2")
    )
    in_specs = (
        P(EXPERT, "dp", None),
        P(EXPERT, "dp", None),
        P(EXPERT, "dp"),
        P(EXPERT, "dp", None),
        P(EXPERT, "dp", None),
        P(EXPERT, "dp", None),
        P(),
        P(),
    )
    out_specs = (
        P(EXPERT, "dp", None),
        P(EXPERT, "dp", None),
        P(EXPERT, "dp", None),
        P(EXPERT, None, None),
    )
    return jax.shard_map(
        on_device, mesh=finer, in_specs=in_specs, out_specs=out_specs, check_vma=False
    )
```

profile of v0, /device:TPU:0, one launch (start us, length us, event | category | flops | bytes accessed | tf_op | source)
XLA Modules:
  0.0 260.9 jit_solution(13356812411573862050)
XLA Ops:
  7.8 9.9 %multiply_convert_fusion = bf16[1536,2048]{1,0:T(8,128)(2,1)S(1)} fusion(bf16[1,1024,2048]{2,1,0:T(8,128)(2,1)} %param.8, bf16[1,1024,1536]{2,1,0:T(8,128)(2,1)} %param.9, pred[1024]{0:T(1024)(128)(4,1)S(1)} %iota_compare_fusion.1), kind=kOutput, calls=%fused_computation.2 | convolution fusion | flops 6450315264 | bytes 13632512 | tf_op jit(solution)/shard_map/dot_general | solution.py:75
  17.7 3.1 %copy.58 = bf16[192,8,8,256]{3,2,0,1:T(8,128)(2,1)} copy(bf16[192,8,8,256]{3,2,1,0:T(8,128)(2,1)S(1)} %bitcast.31) | data formatting | bytes 12582912 | tf_op jit(solution)/shard_map/reshape | solution.py:19
  20.8 8.0 %all-to-all-start = ((bf16[8,256,1536]{1,2,0:T(8,128)(2,1)}), bf16[8,256,1536]{1,2,0:T(8,128)(2,1)}, u32[]{:S(2)}, u32[]{:S(2)}) async-start(bf16[8,256,1536]{1,2,0:T(8,128)(2,1)} %bitcast.30), calls=%async_computation | async-start | bytes 12582912 | tf_op jit(solution)/shard_map/all_to_all | solution.py:25
  28.8 0.0 copy-start.5
  28.8 1.6 copy.46
  30.4 1.6 copy.41
  32.1 3.0 %copy.44 = f32[1,256,1536]{1,2,0:T(8,128)} copy(f32[1,256,1536]{2,1,0:T(8,128)} %param.13) | data formatting | bytes 3145728 | tf_op args[5]
  35.1 67.3 %all-to-all-done = bf16[8,256,1536]{1,2,0:T(8,128)(2,1)} async-done(((bf16[8,256,1536]{1,2,0:T(8,128)(2,1)}), bf16[8,256,1536]{1,2,0:T(8,128)(2,1)}, u32[]{:S(2)}, u32[]{:S(2)}) %all-to-all-start) | async-done | bytes 6291488 | tf_op jit(solution)/shard_map/all_to_all | solution.py:25
  102.3 3.8 %convert_reduce_fusion = f32[256,1536]{0,1:T(8,128)S(1)} fusion(bf16[8,256,1536]{1,2,0:T(8,128)(2,1)} %all-to-all-done), kind=kLoop, calls=%fused_computation.1 | loop fusion | flops 5898240 | bytes 7864320 | tf_op jit(solution)/shard_map/reduce_sum | solution.py:26
  106.1 1.6 copy.48
  107.8 5.9 %multiply_subtract_fusion = (f32[1,256,1536]{1,2,0:T(8,128)}, f32[1,256,1536]{1,2,0:T(8,128)}, f32[1,256,1536]{1,2,0:T(8,128)}, f32[1,256,1536]{1,2,0:T(8,128)}, f32[1,256,1536]{1,2,0:T(8,128)}) fusion(f32[1,256,1536]{1,2,0:T(8,128)} %copy.46, f32[256,1536]{0,1:T(8,128)S(1)} %convert_reduce_fusion, f32[1,256,1536]{1,2,0:T(8,128)} %copy.41, ...), kind=kLoop, calls=%fused_computation.20 | loop fusion | flops 5898240 | bytes 14155776 | tf_op jit(solution)/shard_map/sub | solution.py:61
  113.6 3.0 %copy.49 = f32[1,256,1536]{2,1,0:T(8,128)} copy(f32[1,256,1536]{1,2,0:T(8,128)} %get-tuple-element.20) | data formatting | bytes 3145728 | tf_op jit(solution)/shard_map/mul | solution.py:58
  116.7 3.2 %copy.47 = f32[1,256,1536]{2,1,0:T(8,128)} copy(f32[1,256,1536]{1,2,0:T(8,128)} %get-tuple-element.19) | data formatting | bytes 3145728 | tf_op jit(solution)/shard_map/mul | solution.py:57
  119.8 3.0 %subtract_convert_fusion = bf16[8,2,1,16,1536]{4,3,1,0,2:T(8,128)(2,1)S(1)} fusion(f32[8,2,1,16,1536]{4,3,1,0,2:T(8,128)S(1)} %bitcast.32, f32[8,2,1,16,1536]{4,3,1,0,2:T(8,128)} %bitcast.34, f32[8,2,1,16,1536]{4,3,1,0,2:T(8,128)S(1)} %bitcast.33, f32[8,2,1,16,1536]{4,3,1,0,2:T(8,128)} %bitcast.35), kind=kLoop, calls=%fused_computation.19 | loop fusion | flops 5505024 | bytes 7077888 | tf_op jit(solution)/shard_map/convert_element_type | solution.py:80
  122.8 0.1 copy.50
  122.9 4.4 %all_to_all.27 = bf16[8,2,1,16,1536]{4,3,0,2,1:T(8,128)(2,1)S(1)} all-to-all(bf16[8,2,1,16,1536]{4,3,0,2,1:T(8,128)(2,1)S(1)} %copy.50), channel_id=1, replica_groups=mesh['dp'=8,'expert_0'=4,'expert_1'=2,'expert_2'=2] {'expert_2'}, dimensions={1} | all-to-all | bytes 1572864 | tf_op jit(solution)/shard_map/all_to_all | solution.py:39
  127.3 0.9 copy.51
  128.2 4.5 %all-to-all-start.2 = ((bf16[8,2,1,16,1536]{4,3,1,2,0:T(8,128)(2,1)}), bf16[8,2,1,16,1536]{4,3,1,2,0:T(8,128)(2,1)S(1)}, u32[]{:S(2)}, u32[]{:S(2)}) async-start(bf16[8,2,1,16,1536]{4,3,1,2,0:T(8,128)(2,1)} %copy.51), calls=%async_computation.2 | async-start | bytes 1572864 | tf_op jit(solution)/shard_map/all_to_all | solution.py:39
  132.7 0.0 all-gather.2.cloned.1.call-start
  132.8 0.1 select_reduce_fusion
  132.9 13.0 %all-to-all-done.2 = bf16[8,2,1,16,1536]{4,3,1,2,0:T(8,128)(2,1)S(1)} async-done(((bf16[8,2,1,16,1536]{4,3,1,2,0:T(8,128)(2,1)}), bf16[8,2,1,16,1536]{4,3,1,2,0:T(8,128)(2,1)S(1)}, u32[]{:S(2)}, u32[]{:S(2)}) %all-to-all-start.2) | async-done | bytes 786464 | tf_op jit(solution)/shard_map/all_to_all | solution.py:39
  145.9 0.6 gather_fusion
  146.5 0.1 broadcast_select_fusion
  146.6 0.0 copy-start.3
  146.7 17.1 %all_to_all.28 = bf16[16,16,1536]{2,1,0:T(8,128)(2,1)} all-to-all(bf16[16,16,1536]{2,1,0:T(8,128)(2,1)S(1)} %broadcast_select_fusion), channel_id=1, replica_groups=mesh['dp'=8,'expert_0'=4,'expert_1'=2,'expert_2'=2] {'expert_0','expert_..., dimensions={0} | all-to-all | bytes 1572864 | tf_op jit(solution)/shard_map/all_to_all | solution.py:83
  163.7 0.0 all-gather.2.cloned.1.call-update
  163.7 0.0 copy-start.2
  163.8 1.6 copy.52
  165.4 1.6 copy.53
  167.0 1.6 copy.54
  168.6 79.6 %all-gather.2.cloned.1.call-done = bf16[1,2048,1536]{2,1,0:T(8,128)(2,1)} async-done(((bf16[1,256,1536]{2,1,0:T(8,128)(2,1)}), bf16[1,2048,1536]{2,1,0:T(8,128)(2,1)}) %all-gather.2.cloned.1.call-update) | async-done | bytes 6291472 | tf_op jit(solution)/shard_map/all_gather | solution.py:86
  248.2 5.9 %copy.61 = bf16[1,2048,1536]{2,1,0:T(8,128)(2,1)} copy(bf16[1,2048,1536]{2,1,0:T(8,128)(2,1)} %all-gather.2.cloned.1.call-done) | data formatting | bytes 12582912
  (17 shorter events, 0.1 us)
Async XLA Ops:
  20.8 8.0 %copy-start = (f32[1,256,1536]{2,1,0:T(8,128)S(1)}, f32[1,256,1536]{2,1,0:T(8,128)}, u32[]{:S(2)}) copy-start(f32[1,256,1536]{2,1,0:T(8,128)} %param.11) | copy-start | bytes 4718596
  20.8 81.5 %all-to-all-start = ((bf16[8,256,1536]{1,2,0:T(8,128)(2,1)}), bf16[8,256,1536]{1,2,0:T(8,128)(2,1)}, u32[]{:S(2)}, u32[]{:S(2)}) async-start(bf16[8,256,1536]{1,2,0:T(8,128)(2,1)} %bitcast.30), calls=%async_computation | async-start | bytes 12582912 | tf_op jit(solution)/shard_map/all_to_all | solution.py:25
  28.8 1.6 copy-start.5
  116.7 3.2 %copy-start.4 = (f32[256,1536]{1,0:T(8,128)S(1)}, f32[256,1536]{1,0:T(8,128)}, u32[]{:S(2)}) copy-start(f32[256,1536]{1,0:T(8,128)} %copy.48) | copy-start | bytes 4718596
  127.3 5.5 %copy-start.6 = (s32[16]{0:T(128)S(1)}, s32[16]{0:T(128)}, u32[]{:S(2)}) copy-start(s32[16]{0:T(128)} %param.14) | copy-start | bytes 196
  127.3 5.5 %copy-start.7 = (s32[16]{0:T(128)S(1)}, s32[16]{0:T(128)}, u32[]{:S(2)}) copy-start(s32[16]{0:T(128)} %param.15) | copy-start | bytes 196
  128.2 17.7 %all-to-all-start.2 = ((bf16[8,2,1,16,1536]{4,3,1,2,0:T(8,128)(2,1)}), bf16[8,2,1,16,1536]{4,3,1,2,0:T(8,128)(2,1)S(1)}, u32[]{:S(2)}, u32[]{:S(2)}) async-start(bf16[8,2,1,16,1536]{4,3,1,2,0:T(8,128)(2,1)} %copy.51), calls=%async_computation.2 | async-start | bytes 1572864 | tf_op jit(solution)/shard_map/all_to_all | solution.py:39
  132.7 115.5 %all-gather.2.cloned.1.call-start = ((), (), s32[]{:S(2)}) async-start(), calls=%async_computation.4 | async-start | bytes 7077888 | tf_op jit(solution)/shard_map/all_gather | solution.py:86
  146.6 17.1 %copy-start.3 = (f32[1,256,1536]{1,2,0:T(8,128)S(1)}, f32[1,256,1536]{1,2,0:T(8,128)}, u32[]{:S(2)}) copy-start(f32[1,256,1536]{1,2,0:T(8,128)} %get-tuple-element.16) | copy-start | bytes 4718596
  163.7 1.6 copy-start.2
  165.4 1.6 copy-start.1
Sparse Core Ops, SparseCore 0:
  163.9 84.2 all-gather.1
where the time goes:
time: 261 us
  waiting for transfers between devices  160 us (61%)
  local copies, waits for them, and re-layouts  29.5 us (11%)
  blocking collectives  21.4 us (8%)
  between operations  14.8 us (6%)
  other arithmetic  13 us (5%)
  starting transfers between devices  12.6 us (5%)
  matrix products  9.85 us (4%)
    all_gather x1, waiting for transfers between devices, on_device(): moved = lax.all_gather(placed, 'dp', axis=1, tiled=True)  79.6 us
    all_to_all x1, waiting for transfers between devices, sent_and_summed(): lax.all_to_all(blocks, axis, split_axis=0, concat_axis=0, tiled=True)  67.3 us
    all_to_all x1, blocking collectives, on_device(): lax.all_to_all(jnp.take(spread, source, axis=0), EXPERT, split_axis=0, co...  17.1 us
    unnamed x23, local copies, waits for them, and re-layouts  17 us
    all_to_all x1, waiting for transfers between devices, exchange_in_order(): whole = lax.all_to_all(whole, axes[k], k, k, tiled=True)  13 us
    dot_general x1, matrix products, on_device(): lax.dot_general(inputs, cotangent, (((0,), (0,)), ((), ())), preferred_el...  9.85 us
    all_to_all x1, starting transfers between devices, sent_and_summed(): lax.all_to_all(blocks, axis, split_axis=0, concat_axis=0, tiled=True)  8.02 us
    sub x1, other arithmetic, adamw(): master - learn_rate * (first_hat / (jnp.sqrt(second_hat) + adam_eps) + de...  5.87 us
  transfers between devices with their start and end apart: 3, of which 3 were waited for; matrix products, arithmetic and copies ran while one was open for 4% of the time, Pallas kernels for 0%

commit v1 on v0

--- a/solution.py
+++ b/solution.py
@@ -83,7 +83,9 @@
     placed = lax.all_to_all(
         jnp.take(spread, source, axis=0), EXPERT, split_axis=0, concat_axis=1, tiled=True
     )
-    moved = lax.all_gather(placed, "dp", axis=1, tiled=True)
+    moved = jnp.concatenate(
+        lax.all_to_all(jnp.stack([placed] * lax.axis_size("dp")), "dp", 0, 0), axis=1
+    )
     return (updated[None], first[None], second[None], moved)
 
 

time: 261 us -> 244 us (0.935)
  between operations: 14.8 us -> 1.39 us
  waiting for transfers between devices: 160 us -> 149 us
  starting transfers between devices: 12.6 us -> 17.4 us
  local copies, waits for them, and re-layouts: 29.5 us -> 32.7 us
    all_gather x1 -> x0, waiting for transfers between devices: 79.6 us -> none  [on_device(): moved = lax.all_gather(placed, 'dp', axis=1, tiled=True)]
    all_to_all x0 -> x1, waiting for transfers between devices: none -> 68.6 us  [on_device(): lax.all_to_all(jnp.stack([placed] * lax.axis_size('dp')), 'dp', 0, 0)]
    all_to_all x0 -> x1, starting transfers between devices: none -> 4.88 us  [on_device(): lax.all_to_all(jnp.stack([placed] * lax.axis_size('dp')), 'dp', 0, 0)]
    another operation x0 -> x1, local copies, waits for them, and re-layouts: none -> 3.24 us  [on_device(): jnp.stack([placed] * lax.axis_size('dp'))]
  transfers between devices with their start and end apart: 3 -> 3, of which waited for: 3 -> 3; matrix products, arithmetic and copies ran while one was open for 4% -> 5% of each run, Pallas kernels for 0% -> 0%
where the time goes in v1:
time: 244 us
  waiting for transfers between devices  149 us (61%)
  local copies, waits for them, and re-layouts  32.7 us (13%)
  blocking collectives  20.6 us (8%)
  starting transfers between devices  17.4 us (7%)
  other arithmetic  13 us (5%)
  matrix products  9.85 us (4%)
    all_to_all x1, waiting for transfers between devices, on_device(): lax.all_to_all(jnp.stack([placed] * lax.axis_size('dp')), 'dp', 0, 0)  68.6 us
    all_to_all x1, waiting for transfers between devices, sent_and_summed(): lax.all_to_all(blocks, axis, split_axis=0, concat_axis=0, tiled=True)  67.3 us
    unnamed x23, local copies, waits for them, and re-layouts  17 us
    all_to_all x1, blocking collectives, on_device(): lax.all_to_all(jnp.take(spread, source, axis=0), EXPERT, split_axis=0, co...  16.3 us
    all_to_all x1, waiting for transfers between devices, exchange_in_order(): whole = lax.all_to_all(whole, axes[k], k, k, tiled=True)  13 us
    dot_general x1, matrix products, on_device(): lax.dot_general(inputs, cotangent, (((0,), (0,)), ((), ())), preferred_el...  9.85 us
    all_to_all x1, starting transfers between devices, sent_and_summed(): lax.all_to_all(blocks, axis, split_axis=0, concat_axis=0, tiled=True)  8.02 us
    sub x1, other arithmetic, adamw(): master - learn_rate * (first_hat / (jnp.sqrt(second_hat) + adam_eps) + de...  5.87 us
  transfers between devices with their start and end apart: 3, of which 3 were waited for; matrix products, arithmetic and copies ran while one was open for 5% of the time, Pallas kernels for 0%

profile of v1, /device:TPU:0, one launch (start us, length us, event | category | flops | bytes accessed | tf_op | source)
XLA Modules:
  0.0 243.8 jit_solution(12401348100046426274)
XLA Ops:
  1.3 9.9 %multiply_convert_fusion = bf16[1536,2048]{1,0:T(8,128)(2,1)S(1)} fusion(bf16[1,1024,2048]{2,1,0:T(8,128)(2,1)} %param.8, bf16[1,1024,1536]{2,1,0:T(8,128)(2,1)} %param.9, pred[1024]{0:T(1024)(128)(4,1)S(1)} %iota_compare_fusion.1), kind=kOutput, calls=%fused_computation.2 | convolution fusion | flops 6450315264 | bytes 13632512 | tf_op jit(solution)/shard_map/dot_general | solution.py:75
  11.1 3.1 %copy.58 = bf16[192,8,8,256]{3,2,0,1:T(8,128)(2,1)} copy(bf16[192,8,8,256]{3,2,1,0:T(8,128)(2,1)S(1)} %bitcast.32) | data formatting | bytes 12582912 | tf_op jit(solution)/shard_map/reshape | solution.py:19
  14.3 8.0 %all-to-all-start = ((bf16[8,256,1536]{1,2,0:T(8,128)(2,1)}), bf16[8,256,1536]{1,2,0:T(8,128)(2,1)}, u32[]{:S(2)}, u32[]{:S(2)}) async-start(bf16[8,256,1536]{1,2,0:T(8,128)(2,1)} %bitcast.31), calls=%async_computation | async-start | bytes 12582912 | tf_op jit(solution)/shard_map/all_to_all | solution.py:25
  22.3 0.0 copy-done
  22.3 0.0 copy-start.5
  22.3 1.6 copy.46
  23.9 1.6 copy.41
  25.5 3.0 %copy.44 = f32[1,256,1536]{1,2,0:T(8,128)} copy(f32[1,256,1536]{2,1,0:T(8,128)} %param.13) | data formatting | bytes 3145728 | tf_op args[5]
  28.5 67.3 %all-to-all-done = bf16[8,256,1536]{1,2,0:T(8,128)(2,1)} async-done(((bf16[8,256,1536]{1,2,0:T(8,128)(2,1)}), bf16[8,256,1536]{1,2,0:T(8,128)(2,1)}, u32[]{:S(2)}, u32[]{:S(2)}) %all-to-all-start) | async-done | bytes 6291488 | tf_op jit(solution)/shard_map/all_to_all | solution.py:25
  95.8 3.8 %convert_reduce_fusion = f32[256,1536]{0,1:T(8,128)S(1)} fusion(bf16[8,256,1536]{1,2,0:T(8,128)(2,1)} %all-to-all-done), kind=kLoop, calls=%fused_computation.1 | loop fusion | flops 5898240 | bytes 7864320 | tf_op jit(solution)/shard_map/reduce_sum | solution.py:26
  99.6 1.6 copy.48
  101.2 5.9 %multiply_subtract_fusion = (f32[1,256,1536]{1,2,0:T(8,128)}, f32[1,256,1536]{1,2,0:T(8,128)}, f32[1,256,1536]{1,2,0:T(8,128)}, f32[1,256,1536]{1,2,0:T(8,128)}, f32[1,256,1536]{1,2,0:T(8,128)}) fusion(f32[1,256,1536]{1,2,0:T(8,128)} %copy.46, f32[256,1536]{0,1:T(8,128)S(1)} %convert_reduce_fusion, f32[1,256,1536]{1,2,0:T(8,128)} %copy.41, ...), kind=kLoop, calls=%fused_computation.20 | loop fusion | flops 5898240 | bytes 14155776 | tf_op jit(solution)/shard_map/sub | solution.py:61
  107.1 3.0 %copy.49 = f32[1,256,1536]{2,1,0:T(8,128)} copy(f32[1,256,1536]{1,2,0:T(8,128)} %get-tuple-element.20) | data formatting | bytes 3145728 | tf_op jit(solution)/shard_map/mul | solution.py:58
  110.1 3.1 %copy.47 = f32[1,256,1536]{2,1,0:T(8,128)} copy(f32[1,256,1536]{1,2,0:T(8,128)} %get-tuple-element.19) | data formatting | bytes 3145728 | tf_op jit(solution)/shard_map/mul | solution.py:57
  113.3 3.0 %subtract_convert_fusion = bf16[8,2,1,16,1536]{4,3,1,0,2:T(8,128)(2,1)S(1)} fusion(f32[8,2,1,16,1536]{4,3,1,0,2:T(8,128)S(1)} %bitcast.33, f32[8,2,1,16,1536]{4,3,1,0,2:T(8,128)} %bitcast.35, f32[8,2,1,16,1536]{4,3,1,0,2:T(8,128)S(1)} %bitcast.34, f32[8,2,1,16,1536]{4,3,1,0,2:T(8,128)} %bitcast.36), kind=kLoop, calls=%fused_computation.19 | loop fusion | flops 5505024 | bytes 7077888 | tf_op jit(solution)/shard_map/convert_element_type | solution.py:80
  116.3 0.1 copy.50
  116.3 4.4 %all_to_all.29 = bf16[8,2,1,16,1536]{4,3,0,2,1:T(8,128)(2,1)S(1)} all-to-all(bf16[8,2,1,16,1536]{4,3,0,2,1:T(8,128)(2,1)S(1)} %copy.50), channel_id=1, replica_groups=mesh['dp'=8,'expert_0'=4,'expert_1'=2,'expert_2'=2] {'expert_2'}, dimensions={1} | all-to-all | bytes 1572864 | tf_op jit(solution)/shard_map/all_to_all | solution.py:39
  120.7 0.9 copy.51
  121.6 4.5 %all-to-all-start.2 = ((bf16[8,2,1,16,1536]{4,3,1,2,0:T(8,128)(2,1)}), bf16[8,2,1,16,1536]{4,3,1,2,0:T(8,128)(2,1)S(1)}, u32[]{:S(2)}, u32[]{:S(2)}) async-start(bf16[8,2,1,16,1536]{4,3,1,2,0:T(8,128)(2,1)} %copy.51), calls=%async_computation.2 | async-start | bytes 1572864 | tf_op jit(solution)/shard_map/all_to_all | solution.py:39
  126.1 0.1 select_reduce_fusion
  126.3 13.0 %all-to-all-done.2 = bf16[8,2,1,16,1536]{4,3,1,2,0:T(8,128)(2,1)S(1)} async-done(((bf16[8,2,1,16,1536]{4,3,1,2,0:T(8,128)(2,1)}), bf16[8,2,1,16,1536]{4,3,1,2,0:T(8,128)(2,1)S(1)}, u32[]{:S(2)}, u32[]{:S(2)}) %all-to-all-start.2) | async-done | bytes 786464 | tf_op jit(solution)/shard_map/all_to_all | solution.py:39
  139.3 0.6 gather_fusion
  139.9 0.1 broadcast_select_fusion
  140.1 16.3 %all_to_all.30 = bf16[16,16,1536]{2,1,0:T(8,128)(2,1)S(1)} all-to-all(bf16[16,16,1536]{2,1,0:T(8,128)(2,1)S(1)} %broadcast_select_fusion), channel_id=1, replica_groups=mesh['dp'=8,'expert_0'=4,'expert_1'=2,'expert_2'=2] {'expert_0','expert_..., dimensions={0} | all-to-all | bytes 1572864 | tf_op jit(solution)/shard_map/all_to_all | solution.py:83
  156.4 3.2 %stack.5 = bf16[8,1,256,1536]{3,2,1,0:T(8,128)(2,1)} broadcast(bf16[256,1536]{1,0:T(8,128)(2,1)S(1)} %bitcast.37), dimensions={2,3} | broadcast | bytes 7077888 | tf_op jit(solution)/shard_map/stack | solution.py:87
  159.6 4.9 %all-to-all-start.4 = ((bf16[8,1,256,1536]{3,2,1,0:T(8,128)(2,1)}), bf16[8,1,256,1536]{3,2,1,0:T(8,128)(2,1)}, u32[]{:S(2)}, u32[]{:S(2)}) async-start(bf16[8,1,256,1536]{3,2,1,0:T(8,128)(2,1)} %stack.5), calls=%async_computation.4 | async-start | bytes 12582912 | tf_op jit(solution)/shard_map/all_to_all | solution.py:87
  164.5 0.0 copy-start.2
  164.5 1.6 copy.52
  166.1 1.6 copy.53
  167.7 1.6 copy.54
  169.3 68.6 %all-to-all-done.4 = bf16[8,1,256,1536]{3,2,1,0:T(8,128)(2,1)} async-done(((bf16[8,1,256,1536]{3,2,1,0:T(8,128)(2,1)}), bf16[8,1,256,1536]{3,2,1,0:T(8,128)(2,1)}, u32[]{:S(2)}, u32[]{:S(2)}) %all-to-all-start.4) | async-done | bytes 6291488 | tf_op jit(solution)/shard_map/all_to_all | solution.py:87
  237.9 5.9 %copy.61 = bf16[1,2048,1536]{2,1,0:T(8,128)(2,1)} copy(bf16[1,2048,1536]{2,1,0:T(8,128)(2,1)} %bitcast.13) | data formatting | bytes 12582912
  (17 shorter events, 0.1 us)
Async XLA Ops:
  14.3 8.0 %copy-start = (f32[1,256,1536]{2,1,0:T(8,128)S(1)}, f32[1,256,1536]{2,1,0:T(8,128)}, u32[]{:S(2)}) copy-start(f32[1,256,1536]{2,1,0:T(8,128)} %param.11) | copy-start | bytes 4718596
  14.3 81.5 %all-to-all-start = ((bf16[8,256,1536]{1,2,0:T(8,128)(2,1)}), bf16[8,256,1536]{1,2,0:T(8,128)(2,1)}, u32[]{:S(2)}, u32[]{:S(2)}) async-start(bf16[8,256,1536]{1,2,0:T(8,128)(2,1)} %bitcast.31), calls=%async_computation | async-start | bytes 12582912 | tf_op jit(solution)/shard_map/all_to_all | solution.py:25
  22.3 1.6 copy-start.5
  110.1 3.1 %copy-start.4 = (f32[256,1536]{1,0:T(8,128)S(1)}, f32[256,1536]{1,0:T(8,128)}, u32[]{:S(2)}) copy-start(f32[256,1536]{1,0:T(8,128)} %copy.48) | copy-start | bytes 4718596
  120.7 5.4 %copy-start.6 = (s32[16]{0:T(128)S(1)}, s32[16]{0:T(128)}, u32[]{:S(2)}) copy-start(s32[16]{0:T(128)} %param.14) | copy-start | bytes 196
  120.7 5.4 %copy-start.7 = (s32[16]{0:T(128)S(1)}, s32[16]{0:T(128)}, u32[]{:S(2)}) copy-start(s32[16]{0:T(128)} %param.15) | copy-start | bytes 196
  121.6 17.7 %all-to-all-start.2 = ((bf16[8,2,1,16,1536]{4,3,1,2,0:T(8,128)(2,1)}), bf16[8,2,1,16,1536]{4,3,1,2,0:T(8,128)(2,1)S(1)}, u32[]{:S(2)}, u32[]{:S(2)}) async-start(bf16[8,2,1,16,1536]{4,3,1,2,0:T(8,128)(2,1)} %copy.51), calls=%async_computation.2 | async-start | bytes 1572864 | tf_op jit(solution)/shard_map/all_to_all | solution.py:39
  159.6 4.9 %copy-start.3 = (f32[1,256,1536]{1,2,0:T(8,128)S(1)}, f32[1,256,1536]{1,2,0:T(8,128)}, u32[]{:S(2)}) copy-start(f32[1,256,1536]{1,2,0:T(8,128)} %get-tuple-element.16) | copy-start | bytes 4718596
  159.6 78.4 %all-to-all-start.4 = ((bf16[8,1,256,1536]{3,2,1,0:T(8,128)(2,1)}), bf16[8,1,256,1536]{3,2,1,0:T(8,128)(2,1)}, u32[]{:S(2)}, u32[]{:S(2)}) async-start(bf16[8,1,256,1536]{3,2,1,0:T(8,128)(2,1)} %stack.5), calls=%async_computation.4 | async-start | bytes 12582912 | tf_op jit(solution)/shard_map/all_to_all | solution.py:87
  164.5 1.6 copy-start.2
  166.1 1.6 copy-start.1
